TPU v7x, 128 devices: a whole 4x4x4 slice. The times are simulated.
128 devices in a mesh: ctx: 8 (over y, x_lo), tp: 16 (over x_hi, z, core).
Axes of the slice: x: 4 (x_hi: 2, x_lo: 2; x = x_hi * 2 + x_lo), y: 4, z: 4, core: 2. Of those that a mesh axis runs over, the one named last changes fastest.
Arguments:
- hidden_input: bfloat16 [3072, 8192], P('ctx'), may hold values from -6 to 6
- output_cotangent: bfloat16 [3072, 8192], P('ctx', 'tp'), may hold values from -6 to 6
- query_projection: bfloat16 [8192, 4096], P(None, 'tp')
- key_value_projection: bfloat16 [8192, 2048], P(None, 'tp')
- output_projection: bfloat16 [4096, 8192], P('tp'), may hold values from -0.09375 to 0.09375
- adapter_qkv_down_store: bfloat16 [32, 8192, 192], P('ctx', 'tp'), may hold values from -0.0625 to 0.0625
- adapter_query_up: bfloat16 [32, 64, 4096], P('ctx', None, 'tp'), may hold values from -0.375 to 0.375
- adapter_key_value_up: bfloat16 [32, 64, 2048], P('ctx', None, 'tp'), may hold values from -0.375 to 0.375
- adapter_output_down: bfloat16 [32, 4096, 64], P('ctx', 'tp'), may hold values from -0.1875 to 0.1875
- adapter_output_up: bfloat16 [32, 64, 8192], P('ctx', None, 'tp'), may hold values from -0.75 to 0.75
- crop_token_length: int32 [4], replicated, may hold values from 1 to 2688, 3072 in all
- tenant_per_block: int32 [24], replicated, may hold values from 0 to 31, as said below
- tenant_store_row: int32 [32], replicated, may hold values from 0 to 31, as said below
Outputs:
- output: bfloat16 [3072, 8192], P('ctx', 'tp')
- hidden_input_gradient: bfloat16 [3072, 8192], P('ctx', 'tp')
- grad_down_qkv: float32 [32, 8192, 192], P('ctx', 'tp')
- grad_up_q: float32 [32, 64, 4096], P('ctx', None, 'tp')
- grad_up_kv: float32 [32, 64, 2048], P('ctx', None, 'tp')
- grad_down_o: float32 [32, 4096, 64], P('ctx', 'tp')
- grad_up_o: float32 [32, 64, 8192], P('ctx', None, 'tp')
Inputs may be any that keep to these rules, and one draw needn't show every extreme that they name: A permutation: tenant t's adapters are at store row tenant_store_row[t]; rows j * 4 to (j + 1) * 4 - 1 belong to owner j. `tenant_per_block`: of the 3 blocks of one index of ctx, at most 1 name tenants of one owner, and some owner is named that often.
All inputs are finite; a program needn't handle non-finite values.
Results may differ from a plain program's by a relative error of at most 0.038.
Values may be sent and summed in bfloat16 or wider, within the bound.
A program may use at most 128 MiB of HBM per device.

v0:
```python
import functools
import math

import jax
import jax.numpy as jnp
from jax import lax
from jax.experimental import pallas as pl
from jax.experimental.pallas import tpu as pltpu
from jax.sharding import PartitionSpec as P

HEAD = 128
RANK = 64
BLK = 128
NEG = -1e30
ROPE_BASE = 1000000.0
F32 = jnp.float32
BF16 = jnp.bfloat16
MESH = pl.DeviceIdType.MESH
VMEM = pltpu.VMEM


def nn(a, b):
    return lax.dot_general(a, b, (((1,), (0,)), ((), ())), preferred_element_type=F32)


def nt(a, b):
    return lax.dot_general(a, b, (((1,), (1,)), ((), ())), preferred_element_type=F32)


class Dims:
    def __init__(self, rows, width, heads):
        self.rows = rows
        self.width = width
        self.heads = heads
        self.cols = heads * HEAD
        self.blocks = rows // BLK
        self.dq = slice(0, width)
        self.dk = slice(width, 2 * width)
        self.dv = slice(2 * width, 3 * width)
        at = 3 * width
        self.ou = slice(at, at + width)
        at += width
        self.first = at
        self.qu = slice(at, at + self.cols)
        at += self.cols
        self.kvu = slice(at, at + HEAD)
        at += HEAD
        self.od = slice(at, at + self.cols)
        self.total = at + self.cols

    def late(self, at):
        return slice(at.start - self.first, at.stop - self.first)


def any_spec():
    return pl.BlockSpec(memory_space=pl.ANY)


def vmem_spec():
    return pl.BlockSpec(memory_space=VMEM)


def cost(flops, moved):
    return pl.CostEstimate(flops=int(flops), bytes_accessed=int(moved), transcendentals=0)


def front_body(
    dim,
    n_ctx,
    n_tp,
    tenant,
    store_row,
    down_hbm,
    q_up_hbm,
    kv_up_hbm,
    o_down_hbm,
    o_up_hbm,
    cot,
    x_hbm,
    wq_hbm,
    wkv_hbm,
    maps,
    low_out,
    xq,
    xkv,
    cot_all,
    x_mine,
    x,
    wq,
    wkv,
    down,
    q_up,
    kv_up,
    o_down,
    o_up,
    give_a,
    give_b,
    got_a,
    got_b,
    part,
    recv,
    own,
    load_sem,
    sa_send,
    sa_recv,
    sb_send,
    sb_recv,
    side_send,
    side_recv,
    half_send,
    half_recv,
    cross_send,
    cross_recv,
    ar_send,
    ar_recv,
    br_send,
    br_recv,
):
    c = lax.axis_index("ctx")
    me = lax.axis_index("tp")
    core = lax.rem(me, 2)
    partner = me + 1 - 2 * core
    chip = me // 2
    nz = n_tp // 4
    z = lax.rem(chip, nz)
    xh = chip // nz
    up_z = lax.rem(z + 1, nz)
    down_z = lax.rem(z + nz - 1, nz)
    far_z = lax.rem(z + 2, nz)

    def device(x_at, z_at):
        return (x_at * nz + z_at) * 2 + core

    upper = device(xh, up_z)
    lower = device(xh, down_z)
    opposite = device(1 - xh, z)
    barrier = pltpu.get_barrier_semaphore()
    for k in range(1, n_ctx):
        pl.semaphore_signal(
            barrier, inc=1, device_id=(lax.rem(c + k, n_ctx), me), device_id_type=MESH
        )
    for k in range(1, n_tp):
        pl.semaphore_signal(
            barrier, inc=1, device_id=(c, lax.rem(me + k, n_tp)), device_id_type=MESH
        )
    tenants = down.shape[0]

    def row_of(i, b):
        return store_row[tenant[i * dim.blocks + b]]

    def served(i):
        found = 0
        for b in range(dim.blocks):
            row = row_of(i, b) - c * tenants
            found = found + jnp.where((row >= 0) & (row < tenants), row, 0)
        return found

    stores = [
        pltpu.make_async_copy(source, target, load_sem.at[4 + i])
        for i, (source, target) in enumerate(
            (
                (down_hbm, down),
                (o_up_hbm, o_up),
                (q_up_hbm, q_up),
                (kv_up_hbm, kv_up),
                (o_down_hbm, o_down),
            )
        )
    ]
    for load in stores:
        load.start()
    loads = [
        pltpu.make_async_copy(x_hbm, x, load_sem.at[0]),
        pltpu.make_async_copy(wq_hbm, wq, load_sem.at[1]),
        pltpu.make_async_copy(wkv_hbm, wkv, load_sem.at[2]),
        pltpu.make_async_copy(cot, cot_all.at[me], load_sem.at[3]),
    ]
    for load in loads:
        load.start()

    def fill_first(slot_a, at, row):
        slot_a[at, :, dim.dq] = down[row, 0:RANK, :]
        slot_a[at, :, dim.dk] = down[row, RANK : 2 * RANK, :]
        slot_a[at, :, dim.dv] = down[row, 2 * RANK :, :]
        slot_a[at, :, dim.ou] = o_up[row]

    def fill_late(slot_b, at, row):
        slot_b[at, :, dim.late(dim.qu)] = q_up[row]
        slot_b[at, :, dim.late(dim.kvu)] = kv_up[row]
        slot_b[at, :, dim.late(dim.od)] = o_down[row]

    def hand(k, source, target, send, arrive):
        return pltpu.make_async_remote_copy(
            src_ref=source.at[k],
            dst_ref=target.at[c],
            send_sem=send.at[k],
            recv_sem=arrive.at[k],
            device_id=(lax.rem(c + k, n_ctx), me),
            device_id_type=MESH,
        )

    stores[0].wait()
    stores[1].wait()
    order = [4, 5, 3, 6, 2, 7, 1]
    rows_for = {k: served(lax.rem(c + k, n_ctx)) for k in range(n_ctx)}
    for k in order:
        fill_first(give_a, k, rows_for[k])
        if k == order[0]:
            pl.semaphore_wait(barrier, n_ctx + n_tp - 2)
        hand(k, give_a, got_a, sa_send, sa_recv).start()
    fill_first(got_a, c, rows_for[0])

    def block(line, z_at):
        return device(xh if line == 0 else 1 - xh, z_at)

    def side_copy(way, line):
        source = cot if line == 0 else cot_all.at[block(1, z)]
        return pltpu.make_async_remote_copy(
            src_ref=source,
            dst_ref=cot_all.at[block(line, z)],
            send_sem=side_send.at[way, line],
            recv_sem=side_recv.at[way, line],
            device_id=(c, (upper, lower, opposite)[way]),
            device_id_type=MESH,
        )

    middle = dim.rows // 2
    halves = (slice(0, middle), slice(middle, dim.rows))

    def half_copy(way, line):
        at = block(line, down_z if way == 0 else up_z)
        return pltpu.make_async_remote_copy(
            src_ref=cot_all.at[at, halves[way], :],
            dst_ref=cot_all.at[at, halves[way], :],
            send_sem=half_send.at[way, line],
            recv_sem=half_recv.at[way, line],
            device_id=(c, upper if way == 0 else lower),
            device_id_type=MESH,
        )

    def cross_copy(slot, line, z_at):
        at = block(line, z_at)
        return pltpu.make_async_remote_copy(
            src_ref=cot if slot == 0 else cot_all.at[at],
            dst_ref=cot_all.at[at],
            send_sem=cross_send.at[slot],
            recv_sem=cross_recv.at[slot],
            device_id=(c, partner),
            device_id_type=MESH,
        )

    for way in range(2):
        side_copy(way, 0).start()
    passed = [cross_copy(0, 0, z)]
    passed[0].start()
    for load in stores[2:]:
        load.wait()
    for k in order:
        fill_late(give_b, k, rows_for[k])
    fill_late(got_b, c, rows_for[0])

    def pass_on(line, z_at):
        copy = cross_copy(len(passed), line, z_at)
        copy.start()
        passed.append(copy)

    def relay(line):
        side_copy(0, line).wait_recv()
        half_copy(0, line).start()
        pass_on(line, down_z)
        side_copy(1, line).wait_recv()
        half_copy(1, line).start()
        pass_on(line, up_z)

    for load in loads:
        load.wait()
    depth = x.shape[1]
    step = depth // 8
    xq[...] = jnp.zeros_like(xq)
    xkv[...] = jnp.zeros_like(xkv)

    def project(first, last):
        def one(i, carry):
            at = pl.ds(pl.multiple_of(i * step, step), step)
            xs = x[:, at]
            xq[...] += nn(xs, wq[at, :])
            xkv[...] += nn(xs, wkv[at, :])
            return carry

        lax.fori_loop(first, last, one, 0)

    project(0, 5)
    relay(0)
    project(5, 8)
    side_copy(2, 0).start()
    for k in range(1, n_ctx):
        hand(k, give_a, got_a, sa_send, sa_recv).wait_recv()
    for k in order:
        hand(k, give_b, got_b, sb_send, sb_recv).start()
    owners = [row_of(c, b) // tenants for b in range(dim.blocks)]
    mine = pl.ds(pl.multiple_of(me * dim.width, dim.width), dim.width)
    for b in range(dim.blocks):
        rows = slice(b * BLK, (b + 1) * BLK)
        m = got_a[owners[b]]
        xb = x[rows, mine]
        x_mine[b] = xb
        low = [nt(xb, m[:, at]) for at in (dim.dq, dim.dk, dim.dv)]
        low.append(nt(cot[rows, :], m[:, dim.ou]))
        part[rows, :] = jnp.concatenate(low[:2], axis=1).astype(BF16)
        part[dim.rows + b * BLK : dim.rows + (b + 1) * BLK, :] = jnp.concatenate(
            low[2:], axis=1
        ).astype(BF16)
        maps[b, :, : dim.first] = m
    piece = 2 * dim.rows // n_tp

    def slab(peer):
        return pl.ds(pl.multiple_of(peer * piece, piece), piece)

    def spread(k):
        peer = lax.rem(me + k, n_tp)
        return pltpu.make_async_remote_copy(
            src_ref=part.at[slab(peer), :],
            dst_ref=recv.at[k],
            send_sem=ar_send.at[k],
            recv_sem=ar_recv.at[k],
            device_id=(c, peer),
            device_id_type=MESH,
        )

    def share(k):
        return pltpu.make_async_remote_copy(
            src_ref=own,
            dst_ref=low_out.at[slab(me), :],
            send_sem=br_send.at[k],
            recv_sem=br_recv.at[k],
            device_id=(c, lax.rem(me + k, n_tp)),
            device_id_type=MESH,
        )

    for k in range(1, n_tp):
        spread(k).start()
    side_copy(2, 0).wait_recv()
    for way in range(2):
        side_copy(way, 1).start()
    pass_on(1, z)
    total = part[slab(me), :].astype(F32)
    for k in range(1, n_tp):
        spread(k).wait_recv()
        total = total + recv[k].astype(F32)
    own[...] = total.astype(BF16)
    low_out[slab(me), :] = total.astype(BF16)
    for k in range(1, n_tp):
        share(k).start()
    relay(1)
    for line in range(2):
        for way in range(2):
            half_copy(way, line).wait_recv()
        pass_on(line, far_z)
    for k in range(1, n_ctx):
        hand(k, give_b, got_b, sb_send, sb_recv).wait_recv()
    for b in range(dim.blocks):
        maps[b, :, dim.first :] = got_b[owners[b]]
    for k in range(1, n_tp):
        share(k).wait_recv()
    for k in range(1, n_tp):
        spread(k).wait_send()
        share(k).wait_send()
    for k in range(1, n_ctx):
        hand(k, give_a, got_a, sa_send, sa_recv).wait_send()
        hand(k, give_b, got_b, sb_send, sb_recv).wait_send()
    for way in range(3):
        side_copy(way, 0).wait_send()
    for way in range(2):
        side_copy(way, 1).wait_send()
        for line in range(2):
            half_copy(way, line).wait_send()
    for copy in passed:
        copy.wait()


def front(dim, tenant, store_row, stores, cot, hidden, wq, wkv, collective_id):
    n_ctx = lax.axis_size("ctx")
    n_tp = lax.axis_size("tp")
    sems = pltpu.SemaphoreType.DMA
    rest = dim.total - dim.first
    piece = 2 * dim.rows // n_tp
    return pl.pallas_call(
        functools.partial(front_body, dim, n_ctx, n_tp),
        out_shape=(
            jax.ShapeDtypeStruct((dim.blocks, RANK, dim.total), BF16),
            jax.ShapeDtypeStruct((2 * dim.rows, HEAD), BF16),
            jax.ShapeDtypeStruct((dim.rows, dim.cols), F32),
            jax.ShapeDtypeStruct((dim.rows, HEAD), F32),
            jax.ShapeDtypeStruct((n_tp, dim.rows, dim.width), BF16),
            jax.ShapeDtypeStruct((dim.blocks, BLK, dim.width), BF16),
        ),
        in_specs=[pl.BlockSpec(memory_space=pltpu.SMEM)] * 2
        + [any_spec()] * 5
        + [vmem_spec()]
        + [any_spec()] * 3,
        out_specs=(vmem_spec(),) * 4 + (any_spec(), vmem_spec()),
        scratch_shapes=[
            pltpu.VMEM(hidden.shape, BF16),
            pltpu.VMEM(wq.shape, BF16),
            pltpu.VMEM(wkv.shape, BF16),
        ]
        + [pltpu.VMEM(a.shape, BF16) for a in stores]
        + [
            pltpu.VMEM((n_ctx, RANK, dim.first), BF16),
            pltpu.VMEM((n_ctx, RANK, rest), BF16),
            pltpu.VMEM((n_ctx, RANK, dim.first), BF16),
            pltpu.VMEM((n_ctx, RANK, rest), BF16),
            pltpu.VMEM((2 * dim.rows, HEAD), BF16),
            pltpu.VMEM((n_tp, piece, HEAD), BF16),
            pltpu.VMEM((piece, HEAD), BF16),
            sems((9,)),
            sems((n_ctx,)),
            sems((n_ctx,)),
            sems((n_ctx,)),
            sems((n_ctx,)),
            sems((3, 2)),
            sems((3, 2)),
            sems((2, 2)),
            sems((2, 2)),
            sems((n_tp // 2,)),
            sems((n_tp // 2,)),
            sems((n_tp,)),
            sems((n_tp,)),
            sems((n_tp,)),
            sems((n_tp,)),
        ],
        compiler_params=pltpu.CompilerParams(
            collective_id=collective_id, has_side_effects=True, vmem_limit_bytes=60 << 20
        ),
        cost_estimate=cost(3e10, 1e8),
        name="front",
    )(tenant, store_row, *stores, cot, hidden, wq, wkv)


class SumTp:
    def __init__(self, n, part, out, recv, own, send_a, recv_a, send_b, recv_b):
        self.n = n
        self.part = part
        self.out = out
        self.recv = recv
        self.own = own
        self.sems = (send_a, recv_a, send_b, recv_b)
        self.me = lax.axis_index("tp")
        self.row = lax.axis_index("ctx")
        self.piece = part.shape[0] // n

    def slab(self, peer):
        return pl.ds(pl.multiple_of(peer * self.piece, self.piece), self.piece)

    def spread(self, k):
        peer = lax.rem(self.me + k, self.n)
        return pltpu.make_async_remote_copy(
            src_ref=self.part.at[self.slab(peer), :],
            dst_ref=self.recv.at[k],
            send_sem=self.sems[0].at[k],
            recv_sem=self.sems[1].at[k],
            device_id=(self.row, peer),
            device_id_type=MESH,
        )

    def share(self, k):
        return pltpu.make_async_remote_copy(
            src_ref=self.own,
            dst_ref=self.out.at[self.slab(self.me), :],
            send_sem=self.sems[2].at[k],
            recv_sem=self.sems[3].at[k],
            device_id=(self.row, lax.rem(self.me + k, self.n)),
            device_id_type=MESH,
        )

    def start(self):
        for k in range(1, self.n):
            self.spread(k).start()

    def middle(self):
        total = self.part[self.slab(self.me), :].astype(F32)
        for k in range(1, self.n):
            self.spread(k).wait_recv()
            total = total + self.recv[k].astype(F32)
        self.own[...] = total.astype(self.own.dtype)
        self.out[self.slab(self.me), :] = total.astype(self.out.dtype)
        for k in range(1, self.n):
            self.share(k).start()

    def arrive(self):
        for k in range(1, self.n):
            self.share(k).wait_recv()

    def drain(self):
        for k in range(1, self.n):
            self.spread(k).wait_send()
            self.share(k).wait_send()

    @staticmethod
    def scratch(n, shape, dtype):
        piece = shape[0] // n
        return [
            pltpu.VMEM((n, piece, shape[1]), dtype),
            pltpu.VMEM((piece, shape[1]), dtype),
        ] + [pltpu.SemaphoreType.DMA((n,))] * 4


class ScatterTp:
    def __init__(self, n, product, refs):
        (
            self.away,
            self.cross,
            self.own,
            self.far,
            self.near,
            self.kept,
            self.turn,
            self.last,
            self.cross_send,
            self.cross_recv,
            self.far_send,
            self.far_recv,
            self.near_send,
            self.near_recv,
            self.last_send,
            self.last_recv,
        ) = refs
        self.product = product
        self.chunks = self.own.shape[0]
        rows = self.own.shape[-2]
        self.half = (slice(0, rows // 2), slice(rows // 2, rows))
        self.chips = n // 2
        self.nz = self.chips // 2
        nz = self.nz
        self.row = lax.axis_index("ctx")
        me = lax.axis_index("tp")
        self.core = lax.rem(me, 2)
        chip = me // 2
        self.z = lax.rem(chip, nz)
        self.xh = chip // nz
        self.partner = me + 1 - 2 * self.core
        self.up = lax.rem(self.z + 1, nz)
        self.down = lax.rem(self.z + nz - 1, nz)
        self.across = lax.rem(self.z + 2, nz)
        self.upper = self.device(self.xh, self.up)
        self.lower = self.device(self.xh, self.down)
        self.opposite = self.device(1 - self.xh, self.z)

    def device(self, x_at, z_at):
        return (x_at * self.nz + z_at) * 2 + self.core

    def copy(self, source, target, send, arrive, peer):
        return pltpu.make_async_remote_copy(
            src_ref=source,
            dst_ref=target,
            send_sem=send,
            recv_sem=arrive,
            device_id=(self.row, peer),
            device_id_type=MESH,
        )

    def swap(self, r, zz, xx):
        return self.copy(
            self.away.at[r, zz, xx],
            self.cross.at[r, zz, xx],
            self.cross_send.at[r, zz, xx],
            self.cross_recv.at[r, zz, xx],
            self.partner,
        )

    def multiply(self, r, first, end):
        nz = self.nz

        def one(step, carry):
            shift = jnp.where(
                step < 2, 2, jnp.where(step < 4, 1, jnp.where(step < 6, nz - 1, 0))
            )
            zz = lax.rem(self.z + shift, nz)
            xx = lax.rem(step, 2)
            block = (xx * nz + zz) * 2
            self.away[r, zz, xx] = self.product(r, block + 1 - self.core).astype(BF16)
            self.swap(r, zz, xx).start()
            self.own[r, zz, xx] = self.product(r, block + self.core).astype(BF16)
            return carry

        lax.fori_loop(first, end, one, 0)

    def join(self, r, zz):
        for xx in range(2):
            self.swap(r, zz, xx).wait_recv()
            self.own[r, zz, xx] = (
                self.own[r, zz, xx].astype(F32) + self.cross[r, zz, xx].astype(F32)
            ).astype(BF16)

    def far_copy(self, r, way):
        return self.copy(
            self.own.at[r, self.across, :, self.half[way], :],
            self.far.at[r, way],
            self.far_send.at[r, way],
            self.far_recv.at[r, way],
            self.upper if way == 0 else self.lower,
        )

    def near_copy(self, r, way):
        return self.copy(
            self.own.at[r, self.up if way == 0 else self.down],
            self.near.at[r, way],
            self.near_send.at[r, way],
            self.near_recv.at[r, way],
            self.upper if way == 0 else self.lower,
        )

    def last_copy(self, r):
        return self.copy(
            self.turn.at[r], self.last.at[r], self.last_send.at[r], self.last_recv.at[r], self.opposite
        )

    def go_far(self, r):
        self.join(r, self.across)
        for way in range(2):
            self.far_copy(r, way).start()

    def go_near(self, r):
        for way in range(2):
            zz = self.up if way == 0 else self.down
            self.join(r, zz)
            self.far_copy(r, way).wait_recv()
            half = self.half[way]
            self.own[r, zz, :, half, :] = (
                self.own[r, zz, :, half, :].astype(F32) + self.far[r, way].astype(F32)
            ).astype(BF16)
            self.near_copy(r, way).start()

    def begin(self):
        self.multiply(0, 0, 2)
        self.multiply(1, 0, 2)
        self.go_far(0)
        self.multiply(0, 2, self.chips)
        self.go_far(1)
        self.multiply(1, 2, self.chips)

    def go_last(self, r):
        self.join(r, self.z)
        for way in range(2):
            self.near_copy(r, way).wait_recv()
        for other in (1, 0):
            xx = self.xh if other == 0 else 1 - self.xh
            total = (
                self.own[r, self.z, xx].astype(F32)
                + self.near[r, 0, xx].astype(F32)
                + self.near[r, 1, xx].astype(F32)
            )
            if other == 0:
                self.kept[r] = total
            else:
                self.turn[r] = total.astype(BF16)
                self.last_copy(r).start()

    def total(self, r):
        self.last_copy(r).wait_recv()
        return self.kept[r] + self.last[r].astype(F32)

    def drain(self):
        for r in range(self.chunks):
            for zz in range(self.nz):
                for xx in range(2):
                    self.swap(r, zz, xx).wait_send()
            for way in range(2):
                self.far_copy(r, way).wait_send()
                self.near_copy(r, way).wait_send()
            self.last_copy(r).wait_send()

    count = 16

    @staticmethod
    def scratch(n, rows, wide, chunks):
        nz = n // 4
        sems = pltpu.SemaphoreType.DMA
        return (
            [pltpu.VMEM((chunks, nz, 2, rows, wide), BF16)] * 3
            + [
                pltpu.VMEM((chunks, 2, 2, rows // 2, wide), BF16),
                pltpu.VMEM((chunks, 2, 2, rows, wide), BF16),
                pltpu.VMEM((chunks, rows, wide), F32),
                pltpu.VMEM((chunks, rows, wide), BF16),
                pltpu.VMEM((chunks, rows, wide), BF16),
            ]
            + [sems((chunks, nz, 2))] * 2
            + [sems((chunks, 2))] * 4
            + [sems((chunks,))] * 2
        )


def greet(n_ctx, n_tp):
    c = lax.axis_index("ctx")
    t = lax.axis_index("tp")
    barrier = pltpu.get_barrier_semaphore()
    for k in range(1, n_tp):
        pl.semaphore_signal(
            barrier, inc=1, device_id=(c, lax.rem(t + k, n_tp)), device_id_type=MESH
        )
    for k in range(1, n_ctx):
        pl.semaphore_signal(barrier, inc=1, device_id=(lax.rem(c + k, n_ctx), t), device_id_type=MESH)
    return lambda: pl.semaphore_wait(barrier, n_ctx + n_tp - 2)


def tail_body(
    dim,
    n_ctx,
    n,
    tenant,
    store_row,
    part,
    xs,
    maps,
    gq,
    gkv,
    wq_hbm,
    wkv_hbm,
    o_ref,
    low_grad,
    x_got,
    low_got,
    wq,
    wkv,
    gq_t,
    gkv_t,
    x_give,
    low_give,
    load_sem,
    x_send,
    x_recv,
    low_send,
    low_recv,
    *refs,
):
    row = lax.axis_index("ctx")
    me = lax.axis_index("tp")
    entered = greet(n_ctx, n)
    loads = [
        pltpu.make_async_copy(wq_hbm, wq, load_sem.at[0]),
        pltpu.make_async_copy(wkv_hbm, wkv, load_sem.at[1]),
    ]
    for load in loads:
        load.start()
    sums = SumTp(n, part, low_grad, *refs[:6])
    wide = dim.width // 2

    def product(r, block):
        at = pl.ds(pl.multiple_of(block * dim.width + r * wide, wide), wide)
        return nn(wq[at, :], gq_t[...]) + nn(wkv[at, :], gkv_t[...])

    scatter = ScatterTp(n, product, refs[6:])
    tenants = store_row.shape[0] // n_ctx
    owners = [store_row[tenant[row * dim.blocks + b]] // tenants for b in range(dim.blocks)]

    def chosen(k, values):
        owner = lax.rem(row + k, n_ctx)
        value = values[0]
        for b in range(1, dim.blocks):
            value = jnp.where(owners[b] == owner, values[b], value)
        return value

    def hand(k, source, target, send, arrive):
        return pltpu.make_async_remote_copy(
            src_ref=source.at[k],
            dst_ref=target.at[row],
            send_sem=send.at[k],
            recv_sem=arrive.at[k],
            device_id=(lax.rem(row + k, n_ctx), me),
            device_id_type=MESH,
        )

    def hand_x():
        for k in range(1, n_ctx):
            x_give[k] = chosen(k, [xs[b] for b in range(dim.blocks)])
            hand(k, x_give, x_got, x_send, x_recv).start()
        x_got[row] = chosen(0, [xs[b] for b in range(dim.blocks)])

    def lows(b):
        return jnp.concatenate(
            [
                low_grad[b * BLK : (b + 1) * BLK, :],
                low_grad[dim.rows + b * BLK : dim.rows + (b + 1) * BLK, :],
            ],
            axis=0,
        )

    def hand_low():
        sums.arrive()
        values = [lows(b) for b in range(dim.blocks)]
        for k in range(1, n_ctx):
            low_give[k] = chosen(k, values)
            hand(k, low_give, low_got, low_send, low_recv).start()
        low_got[row] = chosen(0, values)

    def finish(r):
        total = scatter.total(r).T
        cols = slice(r * wide, (r + 1) * wide)
        for b in range(dim.blocks):
            rows = slice(b * BLK, (b + 1) * BLK)
            first = low_grad[rows, :]
            second = low_grad[dim.rows + b * BLK : dim.rows + (b + 1) * BLK, :]

            def columns(at):
                return maps[b, :, at.start + cols.start : at.start + cols.stop]

            low = (
                nn(first[:, :RANK], columns(dim.dq))
                + nn(first[:, RANK:], columns(dim.dk))
                + nn(second[:, :RANK], columns(dim.dv))
            )
            o_ref[rows, cols] = (total[rows, :] + low).astype(BF16)

    gq_t[...] = gq[...].T
    gkv_t[...] = gkv[...].T
    entered()
    sums.start()
    for load in loads:
        load.wait()
    scatter.begin()
    hand_x()
    sums.middle()
    for r in range(2):
        scatter.go_near(r)
    hand_low()
    for r in range(2):
        scatter.go_last(r)
    for r in range(2):
        finish(r)
    for k in range(1, n_ctx):
        hand(k, x_give, x_got, x_send, x_recv).wait()
        hand(k, low_give, low_got, low_send, low_recv).wait()
    sums.drain()
    scatter.drain()


def tail(dim, tenant, store_row, part, xs, maps, grad_q, grad_kv, wq, wkv, collective_id):
    n = lax.axis_size("tp")
    n_ctx = lax.axis_size("ctx")
    low_shape = (n_ctx, 2 * BLK, HEAD)
    smem = pl.BlockSpec(memory_space=pltpu.SMEM)
    sems = pltpu.SemaphoreType.DMA
    return pl.pallas_call(
        functools.partial(tail_body, dim, n_ctx, n),
        out_shape=(
            jax.ShapeDtypeStruct((dim.rows, dim.width), BF16),
            jax.ShapeDtypeStruct(part.shape, BF16),
            jax.ShapeDtypeStruct((n_ctx, BLK, dim.width), BF16),
            jax.ShapeDtypeStruct(low_shape, BF16),
        ),
        in_specs=[smem, smem] + [vmem_spec()] * 5 + [any_spec()] * 2,
        out_specs=(vmem_spec(),) * 4,
        scratch_shapes=[
            pltpu.VMEM(wq.shape, BF16),
            pltpu.VMEM(wkv.shape, BF16),
            pltpu.VMEM(grad_q.shape[::-1], BF16),
            pltpu.VMEM(grad_kv.shape[::-1], BF16),
            pltpu.VMEM((n_ctx, BLK, dim.width), BF16),
            pltpu.VMEM(low_shape, BF16),
            sems((2,)),
        ]
        + [sems((n_ctx,))] * 4
        + SumTp.scratch(n, part.shape, BF16)
        + ScatterTp.scratch(n, dim.width // 2, dim.rows, 2),
        compiler_params=pltpu.CompilerParams(
            collective_id=collective_id, has_side_effects=True, vmem_limit_bytes=60 << 20
        ),
        cost_estimate=cost(3e10, 1e8),
        name="tail",
    )(tenant, store_row, part, xs, maps, grad_q, grad_kv, wq, wkv)


def finalize_body(dim, xq, xkv, low, maps, ctab, stab, q_out, kv_out, delta_out):
    core = lax.rem(lax.axis_index("tp"), 2)
    is_value = core == 1
    for b in range(dim.blocks):
        rows = slice(b * BLK, (b + 1) * BLK)
        m = maps.at[b]
        first = low[0, rows, :]
        second = low[1, rows, :]
        low_q = first[:, :RANK]
        low_kv = jnp.where(is_value, second[:, :RANK], first[:, RANK:])
        low_o = second[:, RANK:]
        cosine = ctab[rows, :]
        sine = stab[rows, :]
        delta_out[rows, :] = nn(low_o, m[:, dim.od])
        turn = xq[rows, :] + nn(low_q, m[:, dim.qu])
        for head in range(dim.heads):
            cols = slice(head * HEAD, (head + 1) * HEAD)
            q = turn[:, cols]
            q_out[rows, cols] = (q * cosine + pltpu.roll(q, HEAD // 2, 1) * sine).astype(BF16)
        kv = xkv[rows, :] + nn(low_kv, m[:, dim.kvu])
        kv = kv.astype(BF16).astype(F32)
        turned = kv * cosine + pltpu.roll(kv, HEAD // 2, 1) * sine
        kv_out[rows, :] = jnp.where(is_value, kv, turned).astype(BF16)


def finalize(dim, xq, xkv, low, maps, ctab, stab):
    cols = dim.heads * HEAD
    return pl.pallas_call(
        functools.partial(finalize_body, dim),
        out_shape=(
            jax.ShapeDtypeStruct((dim.rows, cols), BF16),
            jax.ShapeDtypeStruct((dim.rows, HEAD), BF16),
            jax.ShapeDtypeStruct((dim.rows, cols), F32),
        ),
        in_specs=[vmem_spec()] * 6,
        out_specs=(vmem_spec(),) * 3,
        cost_estimate=cost(1e8, 4e6),
        name="finalize",
    )(xq, xkv, low, maps, ctab, stab)


def gather_kv_body(n, x_ref, o_ref, send_a, recv_a, send_b, recv_b):
    c = lax.axis_index("ctx")
    t = lax.axis_index("tp")
    core = lax.rem(t, 2)
    partner = t + 1 - 2 * core
    barrier = pltpu.get_barrier_semaphore()
    pl.semaphore_signal(barrier, inc=1, device_id=(c, partner), device_id_type=MESH)
    for k in range(1, n):
        pl.semaphore_signal(barrier, inc=1, device_id=(lax.rem(c + k, n), t), device_id_type=MESH)
    pl.semaphore_wait(barrier, n)
    copies = []
    for k in range(1, n):
        copy = pltpu.make_async_remote_copy(
            src_ref=x_ref,
            dst_ref=o_ref.at[core, c],
            send_sem=send_a.at[k],
            recv_sem=recv_a.at[k],
            device_id=(lax.rem(c + k, n), t),
            device_id_type=MESH,
        )
        copy.start()
        copies.append(copy)
    forwards = []
    copy = pltpu.make_async_remote_copy(
        src_ref=x_ref,
        dst_ref=o_ref.at[core, c],
        send_sem=send_b.at[0],
        recv_sem=recv_b.at[0],
        device_id=(c, partner),
        device_id_type=MESH,
    )
    copy.start()
    forwards.append(copy)
    o_ref[core, c] = x_ref[...]
    for k in range(1, n):
        source = lax.rem(c - k + n, n)
        copies[k - 1].wait_recv()
        copy = pltpu.make_async_remote_copy(
            src_ref=o_ref.at[core, source],
            dst_ref=o_ref.at[core, source],
            send_sem=send_b.at[k],
            recv_sem=recv_b.at[k],
            device_id=(c, partner),
            device_id_type=MESH,
        )
        copy.start()
        forwards.append(copy)
    for k in range(1, n):
        copies[k - 1].wait_send()
    for copy in forwards:
        copy.wait()


def gather_kv(kv, collective_id):
    n = lax.axis_size("ctx")
    rows = kv.shape[0]
    return pl.pallas_call(
        functools.partial(gather_kv_body, n),
        out_shape=jax.ShapeDtypeStruct((2, n, rows, HEAD), BF16),
        in_specs=[vmem_spec()],
        out_specs=vmem_spec(),
        scratch_shapes=[pltpu.SemaphoreType.DMA((n,))] * 4,
        compiler_params=pltpu.CompilerParams(collective_id=collective_id, has_side_effects=True),
        cost_estimate=cost(3e9, 3e7),
        name="gather_kv",
    )(kv)


def allowed_tile(j, rows, first_pos, start):
    key_pos = j * rows + lax.broadcasted_iota(jnp.int32, (rows, rows), 0)
    query_pos = first_pos + lax.broadcasted_iota(jnp.int32, (1, rows), 1)
    return (key_pos <= query_pos) & (key_pos >= start)


def attend_body(dim, meta, start_ref, q_ref, kv_ref, maps, o_ref, lse_ref, part, s_scr, acc):
    rows = dim.rows
    scale = HEAD ** (-0.5)
    lo = meta[0]
    hi = meta[1]
    first_pos = meta[2]
    start = start_ref[...]
    heads = range(dim.heads)

    def scores(j, peaks):
        kj = kv_ref[0, j]
        ok = allowed_tile(j, rows, first_pos, start)
        fresh = []
        for h in heads:
            s = nt(kj, q_ref[:, h * HEAD : (h + 1) * HEAD]) * scale
            s = jnp.where(ok, s, NEG)
            s_scr[h, j] = s
            fresh.append(jnp.maximum(peaks[h], jnp.max(s, axis=0, keepdims=True)))
        return tuple(fresh)

    peaks = lax.fori_loop(lo, hi, scores, tuple(jnp.full((1, rows), NEG, F32) for h in heads))
    acc[...] = jnp.zeros_like(acc)

    def mix(j, sums):
        vt = kv_ref[1, j].T
        fresh = []
        for h in heads:
            p = jnp.exp(s_scr[h, j] - peaks[h])
            fresh.append(sums[h] + jnp.sum(p, axis=0, keepdims=True))
            acc[h] += nn(vt, p.astype(BF16))
        return tuple(fresh)

    sums = lax.fori_loop(lo, hi, mix, tuple(jnp.zeros((1, rows), F32) for h in heads))
    for h in heads:
        o_ref[:, h * HEAD : (h + 1) * HEAD] = (acc[h] / sums[h]).T.astype(BF16)
        lse_ref[h] = peaks[h] + jnp.log(sums[h])
    for b in range(dim.blocks):
        at = slice(b * BLK, (b + 1) * BLK)
        part[at, :] = nt(o_ref[at, :], maps[b, :, dim.od])


def attend(dim, meta, start, q, kv, maps):
    n = kv.shape[1]
    rows = dim.rows
    return pl.pallas_call(
        functools.partial(attend_body, dim),
        out_shape=(
            jax.ShapeDtypeStruct(q.shape, BF16),
            jax.ShapeDtypeStruct((dim.heads, 1, rows), F32),
            jax.ShapeDtypeStruct((rows, RANK), F32),
        ),
        in_specs=[pl.BlockSpec(memory_space=pltpu.SMEM)] + [vmem_spec()] * 4,
        out_specs=(vmem_spec(),) * 3,
        scratch_shapes=[
            pltpu.VMEM((dim.heads, n, rows, rows), F32),
            pltpu.VMEM((dim.heads, HEAD, rows), F32),
        ],
        compiler_params=pltpu.CompilerParams(vmem_limit_bytes=40 << 20),
        cost_estimate=cost(4 * dim.heads * rows * rows * n * HEAD * 4, 3e7),
        name="attend",
    )(meta, start, q, kv, maps)


def back_body(
    dim,
    n_ctx,
    n_tp,
    start_ref,
    q_ref,
    kv_ref,
    o_ref,
    lse_ref,
    low_part,
    o_delta,
    ctab,
    stab,
    maps,
    cot_hbm,
    wo_hbm,
    out_ref,
    dq_ref,
    gkv_ref,
    low_out,
    cot_ref,
    wo_ref,
    dkv_ref,
    acc,
    grad,
    do_ref,
    half,
    mine,
    arrived,
    load_sem,
    send_a,
    recv_a,
    send_b,
    recv_b,
    *refs,
):
    c = lax.axis_index("ctx")
    t = lax.axis_index("tp")
    core = lax.rem(t, 2)
    partner = t + 1 - 2 * core
    rows = dim.rows
    scale = HEAD ** (-0.5)
    heads = range(dim.heads)
    entered = greet(n_ctx, n_tp)
    load_wo = pltpu.make_async_copy(wo_hbm, wo_ref, load_sem.at[0])
    load_cot = pltpu.make_async_copy(cot_hbm, cot_ref, load_sem.at[1])
    load_wo.start()
    load_cot.start()
    sums = SumTp(n_tp, low_part, low_out, *refs[:6])
    wide = dim.width // 2

    def product(r, block):
        at = block * dim.width + r * wide
        return nn(o_ref[...], wo_ref[:, pl.ds(pl.multiple_of(at, wide), wide)])

    scatter = ScatterTp(n_tp, product, refs[6:])
    entered()
    sums.start()
    load_wo.wait()
    scatter.begin()
    sums.middle()

    load_cot.wait()
    grad[...] = o_delta[...]

    def features(g, carry):
        at = pl.ds(pl.multiple_of(g * dim.width, dim.width), dim.width)
        grad[...] += nt(cot_ref[g], wo_ref[:, at])
        return carry

    middle = n_tp // 2
    lax.fori_loop(0, middle, features, 0)
    for r in range(scatter.chunks):
        scatter.go_near(r)
    lax.fori_loop(middle, n_tp, features, 0)
    do_ref[...] = grad[...].astype(BF16)

    start = start_ref[...]
    acc[...] = jnp.zeros_like(acc)

    def clear(j, carry):
        dkv_ref[0, j] = jnp.zeros((rows, HEAD), BF16)
        dkv_ref[1, j] = jnp.zeros((rows, HEAD), BF16)
        return carry

    lax.fori_loop(c + 1, n_ctx, clear, 0)
    delta = []
    for h in heads:
        cols = slice(h * HEAD, (h + 1) * HEAD)
        both = do_ref[:, cols].astype(F32) * o_ref[:, cols].astype(F32)
        delta.append(jnp.sum(both.T, axis=0, keepdims=True))

    def step(j, carry):
        kj = kv_ref[0, j]
        vj = kv_ref[1, j]
        kt = kj.T
        ok = allowed_tile(j, rows, c * rows, start)
        dk = jnp.zeros((rows, HEAD), F32)
        dv = jnp.zeros((rows, HEAD), F32)
        for h in heads:
            qh = q_ref[:, h * HEAD : (h + 1) * HEAD]
            doh = do_ref[:, h * HEAD : (h + 1) * HEAD]
            s = jnp.where(ok, nt(kj, qh) * scale, NEG)
            p = jnp.exp(s - lse_ref[h])
            ds = (p * (nt(vj, doh) - delta[h])).astype(BF16)
            acc[h] += nn(kt, ds)
            dk += nn(ds, qh)
            dv += nn(p.astype(BF16), doh)
        dkv_ref[0, j] = (dk * scale).astype(BF16)
        dkv_ref[1, j] = dv.astype(BF16)
        return carry

    lax.fori_loop(0, c + 1, step, 0)

    order = list(range(1, n_ctx)) + [0]

    def swap(k):
        return pltpu.make_async_remote_copy(
            src_ref=dkv_ref.at[1 - core, lax.rem(c + k, n_ctx)],
            dst_ref=half.at[k],
            send_sem=send_a.at[k],
            recv_sem=recv_a.at[k],
            device_id=(c, partner),
            device_id_type=MESH,
        )

    def send(k):
        return pltpu.make_async_remote_copy(
            src_ref=mine.at[k],
            dst_ref=arrived.at[k],
            send_sem=send_b.at[k],
            recv_sem=recv_b.at[k],
            device_id=(lax.rem(c + k, n_ctx), t),
            device_id_type=MESH,
        )

    for k in order:
        swap(k).start()
    for h in heads:
        dq = (acc[h] * scale).T
        dq = dq * ctab[...] - pltpu.roll(dq, HEAD // 2, 1) * stab[...]
        dq_ref[:, h * HEAD : (h + 1) * HEAD] = dq.astype(BF16)
    for k in range(1, n_ctx):
        swap(k).wait_recv()
        mine[k] = (
            dkv_ref[core, lax.rem(c + k, n_ctx)].astype(F32) + half[k].astype(F32)
        ).astype(BF16)
        send(k).start()
    for r in range(scatter.chunks):
        scatter.go_last(r)
    sums.arrive()
    for r in range(scatter.chunks):
        total = scatter.total(r)
        cols = slice(r * wide, (r + 1) * wide)
        for b in range(dim.blocks):
            at = slice(b * BLK, (b + 1) * BLK)
            low = nn(
                low_out[at, :].astype(BF16),
                maps[b, :, dim.ou.start + cols.start : dim.ou.start + cols.stop],
            )
            out_ref[at, cols] = (total[at, :] + low).astype(BF16)
    swap(0).wait_recv()
    total = dkv_ref[core, c].astype(F32) + half[0].astype(F32)
    for k in range(1, n_ctx):
        send(k).wait_recv()
        total = total + arrived[k].astype(F32)
    turned = total * ctab[...] - pltpu.roll(total, HEAD // 2, 1) * stab[...]
    gkv_ref[...] = jnp.where(core == 1, total, turned).astype(BF16)
    for k in order:
        swap(k).wait_send()
    for k in range(1, n_ctx):
        send(k).wait_send()
    sums.drain()
    scatter.drain()


def back(dim, start, q, kv, out, lse, low_part, o_delta, ctab, stab, maps, cot_all, wo, collective_id):
    n_ctx = lax.axis_size("ctx")
    n_tp = lax.axis_size("tp")
    rows = dim.rows
    sems = pltpu.SemaphoreType.DMA
    return pl.pallas_call(
        functools.partial(back_body, dim, n_ctx, n_tp),
        out_shape=(
            jax.ShapeDtypeStruct((rows, dim.width), BF16),
            jax.ShapeDtypeStruct(q.shape, BF16),
            jax.ShapeDtypeStruct((rows, HEAD), BF16),
            jax.ShapeDtypeStruct(low_part.shape, F32),
        ),
        in_specs=[vmem_spec()] * 10 + [any_spec()] * 2,
        out_specs=(vmem_spec(),) * 4,
        scratch_shapes=[
            pltpu.VMEM(cot_all.shape, BF16),
            pltpu.VMEM(wo.shape, BF16),
            pltpu.VMEM(kv.shape, BF16),
            pltpu.VMEM((dim.heads, HEAD, rows), F32),
            pltpu.VMEM((rows, dim.cols), F32),
            pltpu.VMEM((rows, dim.cols), BF16),
            pltpu.VMEM((n_ctx, rows, HEAD), BF16),
            pltpu.VMEM((n_ctx, rows, HEAD), BF16),
            pltpu.VMEM((n_ctx, rows, HEAD), BF16),
            sems((2,)),
        ]
        + [sems((n_ctx,))] * 4
        + SumTp.scratch(n_tp, low_part.shape, F32)
        + ScatterTp.scratch(n_tp, rows, dim.width // 2, 2),
        compiler_params=pltpu.CompilerParams(
            collective_id=collective_id, has_side_effects=True, vmem_limit_bytes=60 << 20
        ),
        cost_estimate=cost(3e10, 1e8),
        name="back",
    )(start, q, kv, out, lse, low_part, o_delta, ctab, stab, maps, cot_all, wo)


def middle_body(
    dim, index_ref, cot, low_in, low_out_ref, attn, grad_q, grad_kv, maps, part, out
):
    core = lax.rem(lax.axis_index("tp"), 2)
    m = maps.at[0]
    low_q = nt(grad_q[...], m[:, dim.qu])
    low_kv = nt(grad_kv[...], m[:, dim.kvu])
    zero = jnp.zeros_like(low_kv)
    part[0] = jnp.concatenate([low_q, jnp.where(core == 0, low_kv, zero)], axis=1).astype(BF16)
    part[1] = jnp.concatenate([jnp.where(core == 1, low_kv, zero), zero], axis=1).astype(BF16)
    first_t = low_in[0].T
    second_t = low_in[1].T
    low_kv_t = jnp.where(core == 1, second_t[:RANK], first_t[RANK:])
    base = dim.ou.start

    def put(at, value):
        out[0, :, at.start - base : at.stop - base] = value.astype(BF16)

    put(dim.ou, nn(low_out_ref[...].T.astype(BF16), cot[...]))
    put(dim.qu, nn(first_t[:RANK], grad_q[...]))
    put(dim.kvu, nn(low_kv_t, grad_kv[...]))
    put(dim.od, nn(second_t[RANK:], attn[...]))


def middle(dim, index, owners, cot, low_in, low_out, attn, grad_q, grad_kv, maps):
    small = dim.total - dim.ou.start
    low_spec = pl.BlockSpec((2, BLK, HEAD), lambda b, idx: (0, b, 0))

    def rows_spec(width):
        return pl.BlockSpec((BLK, width), lambda b, idx: (b, 0))

    return pl.pallas_call(
        functools.partial(middle_body, dim),
        out_shape=(
            jax.ShapeDtypeStruct((2, dim.rows, HEAD), BF16),
            jax.ShapeDtypeStruct((owners, RANK, small), BF16),
        ),
        grid_spec=pltpu.PrefetchScalarGridSpec(
            num_scalar_prefetch=1,
            grid=(dim.blocks,),
            in_specs=[
                rows_spec(dim.width),
                low_spec,
                rows_spec(RANK),
                rows_spec(dim.cols),
                rows_spec(dim.cols),
                rows_spec(HEAD),
                pl.BlockSpec((1, RANK, dim.total), lambda b, idx: (b, 0, 0)),
            ],
            out_specs=(
                low_spec,
                pl.BlockSpec((1, RANK, small), lambda b, idx: (idx[b], 0, 0)),
            ),
        ),
        cost_estimate=cost(1e9, 6e6),
        name="middle",
    )(index, cot, low_in, low_out, attn, grad_q, grad_kv, maps)


def store_body(dim, row_ref, arrived, x_got, low_got, down, q_up, kv_up, o_down, o_up):
    i = pl.program_id(0)

    @pl.when(i == 0)
    def _():
        for ref in (down, q_up, kv_up, o_down, o_up):
            ref[...] = jnp.zeros_like(ref)

    row = row_ref[i]

    @pl.when(row >= 0)
    def _():
        base = dim.ou.start

        def piece(at):
            return arrived[0, :, at.start - base : at.stop - base].astype(F32)

        x = x_got[0]
        down[row, 0 : 2 * RANK, :] += nn(low_got[0, :BLK, :].T, x)
        down[row, 2 * RANK :, :] += nn(low_got[0, BLK:, :].T[:RANK], x)
        q_up[row] += piece(dim.qu)
        kv_up[row] += piece(dim.kvu)
        o_down[row] += piece(dim.od)
        o_up[row] += piece(dim.ou)


def to_store(dim, rows, arrived, x_got, low_got, shapes):
    count = arrived.shape[0]

    def whole(shape):
        return pl.BlockSpec(shape, lambda i, idx: (0, 0, 0))

    def one(array):
        return pl.BlockSpec((1,) + array.shape[1:], lambda i, idx: (i, 0, 0))

    return pl.pallas_call(
        functools.partial(store_body, dim),
        out_shape=tuple(jax.ShapeDtypeStruct(s, F32) for s in shapes),
        grid_spec=pltpu.PrefetchScalarGridSpec(
            num_scalar_prefetch=1,
            grid=(count,),
            in_specs=[one(arrived), one(x_got), one(low_got)],
            out_specs=tuple(whole(s) for s in shapes),
        ),
        cost_estimate=cost(0, 6e6),
        name="to_store",
    )(rows, arrived, x_got, low_got)


def body(
    hidden_input,
    output_cotangent,
    query_projection,
    key_value_projection,
    output_projection,
    adapter_qkv_down_store,
    adapter_query_up,
    adapter_key_value_up,
    adapter_output_down,
    adapter_output_up,
    crop_token_length,
    tenant_per_block,
    tenant_store_row,
):
    ctx_count = lax.axis_size("ctx")
    ctx_index = lax.axis_index("ctx")
    tp_index = lax.axis_index("tp")
    rows_dev = hidden_input.shape[0]
    out_cols = output_cotangent.shape[1]
    tenants = adapter_qkv_down_store.shape[0]
    dim = Dims(rows_dev, out_cols, query_projection.shape[1] // HEAD)
    stores = (
        jnp.swapaxes(adapter_qkv_down_store, 1, 2),
        adapter_query_up,
        adapter_key_value_up,
        jnp.swapaxes(adapter_output_down, 1, 2),
        adapter_output_up,
    )

    tenant_ids = jnp.arange(tenant_store_row.shape[0], dtype=jnp.int32)
    rows_per_block = jnp.sum(
        jnp.where(tenant_per_block[:, None] == tenant_ids[None, :], tenant_store_row[None, :], 0),
        axis=1,
    )
    shard_rows = rows_per_block.reshape(ctx_count, dim.blocks)
    shard_owner = shard_rows // tenants
    served = shard_owner == ctx_index
    served_row = jnp.max(jnp.where(served, shard_rows - ctx_index * tenants, -1), axis=1)
    my_owner = lax.dynamic_index_in_dim(shard_owner, ctx_index, 0, keepdims=False)

    my_pos = ctx_index * rows_dev + jnp.arange(rows_dev, dtype=jnp.int32)
    crop_ends = jnp.cumsum(crop_token_length)
    row_start = jnp.max(
        jnp.where(crop_ends[:, None] <= my_pos[None, :], crop_ends[:, None], 0), axis=0
    ).astype(jnp.int32)
    first_pos = ctx_index * rows_dev
    first_start = jnp.max(jnp.where(crop_ends <= first_pos, crop_ends, 0))
    meta = jnp.stack([first_start // rows_dev, ctx_index + 1, first_pos]).astype(jnp.int32)
    start = row_start[None, :]
    half_dim = HEAD // 2
    exponent = jnp.arange(half_dim, dtype=F32) * (2.0 / HEAD)
    frequency = jnp.exp(-exponent * math.log(ROPE_BASE))
    angles = my_pos.astype(F32)[:, None] * jnp.concatenate([frequency, frequency])[None, :]
    sign = jnp.where(jnp.arange(HEAD) < half_dim, -1.0, 1.0).astype(F32)
    ctab = jnp.cos(angles)
    stab = jnp.sin(angles) * sign[None, :]

    maps, low_in, xq, xkv, cot_all, x_mine = front(
        dim,
        tenant_per_block,
        tenant_store_row,
        stores,
        output_cotangent,
        hidden_input,
        query_projection,
        key_value_projection,
        5,
    )
    low_in = low_in.reshape(2, rows_dev, HEAD)
    query, keyval, o_delta = finalize(dim, xq, xkv, low_in, maps, ctab, stab)
    kv_all = gather_kv(keyval, 1)
    attn, lse, low_part = attend(dim, meta, start, query, kv_all, maps)

    output, grad_q, grad_kv, low_out = back(
        dim,
        start,
        query,
        kv_all,
        attn,
        lse,
        low_part,
        o_delta,
        ctab,
        stab,
        maps,
        cot_all,
        output_projection,
        2,
    )
    low_grad_part, sent = middle(
        dim, my_owner, ctx_count, output_cotangent, low_in, low_out, attn, grad_q, grad_kv, maps
    )
    hidden_input_gradient, unused, x_got, low_got = tail(
        dim,
        tenant_per_block,
        tenant_store_row,
        low_grad_part.reshape(2 * rows_dev, HEAD),
        x_mine,
        maps,
        grad_q,
        grad_kv,
        query_projection,
        key_value_projection,
        3,
    )
    returned = lax.all_to_all(sent, "ctx", split_axis=0, concat_axis=0, tiled=True)
    grads = to_store(dim, served_row, returned, x_got, low_got, [s.shape for s in stores])
    return (
        output,
        hidden_input_gradient,
        jnp.swapaxes(grads[0], 1, 2),
        grads[1],
        grads[2],
        jnp.swapaxes(grads[3], 1, 2),
        grads[4],
    )


def solution(mesh):
    in_specs = (
        P("ctx", None),
        P("ctx", "tp"),
        P(None, "tp"),
        P(None, "tp"),
        P("tp", None),
        P("ctx", "tp", None),
        P("ctx", None, "tp"),
        P("ctx", None, "tp"),
        P("ctx", "tp", None),
        P("ctx", None, "tp"),
        P(),
        P(),
        P(),
    )
    out_specs = (
        P("ctx", "tp"),
        P("ctx", "tp"),
        P("ctx", "tp", None),
        P("ctx", None, "tp"),
        P("ctx", None, "tp"),
        P("ctx", "tp", None),
        P("ctx", None, "tp"),
    )
    return jax.shard_map(body, mesh=mesh, in_specs=in_specs, out_specs=out_specs, check_vma=False)
```

profile of v0, /device:TPU:0, one launch (start us, length us, event | category | flops | bytes accessed | tf_op | source)
XLA Modules:
  0.0 231.7 jit_solution(14700525038128540537)
XLA Ops:
  0.6 0.8 reduce-window.8
  1.5 0.6 fusion.4
  4.1 0.1 compare_select_fusion.1
  4.2 0.9 select_reduce_fusion
  5.0 1.5 fusion
  6.5 65.1 %front.1 = (bf16[3,64,2688]{2,1,0:T(8,128)(2,1)}, bf16[768,128]{1,0:T(8,128)(2,1)}, f32[384,256]{1,0:T(8,128)}, f32[384,128]{1,0:T(8,128)}, bf16[16,384,512]{2,1,0:T(8,128)(2,1)}, /*index=5*/bf16[3,128,512]{2,1,0:T(8,128)(2,1)}) custom-call(s32[24]{0:T(128)} %tenant.3, s32[32]{0:T(128)} %store_row.3, bf16[4,192,512]{2,1,0:T(8,128)(2,1)} %bitcast.18, ...), custom_call_target="tpu_custom_call" | custom-call | flops 30000001024 | bytes 100000000 | tf_op jit(solution)/shard_map/front/pallas_call | solution.py:387
  71.7 2.8 %finalize.1 = (bf16[384,256]{1,0:T(8,128)(2,1)}, bf16[384,128]{1,0:T(8,128)(2,1)}, f32[384,256]{1,0:T(8,128)}) custom-call(f32[384,256]{1,0:T(8,128)} %get-tuple-element.33.xq, f32[384,128]{1,0:T(8,128)} %get-tuple-element.34.xkv, bf16[2,384,128]{2,1,0:T(8,128)(2,1)} %bitcast.14, bf16[3,64,2688]{2,1,0:T(8,128)(2,1)} %get-tuple-element.36.maps, ...), custom_call_target="tpu_custom_call" | custom-call | flops 100000000 | bytes 4000000 | tf_op jit(solution)/shard_map/finalize/pallas_call | solution.py:901
  74.5 17.5 %gather_kv.1.kv_ref = bf16[2,8,384,128]{3,2,1,0:T(8,128)(2,1)} custom-call(bf16[384,128]{1,0:T(8,128)(2,1)} %get-tuple-element.38.x_ref), custom_call_target="tpu_custom_call" | custom-call | flops 3000000000 | bytes 30000000 | tf_op jit(solution)/shard_map/gather_kv/pallas_call | solution.py:971
  92.0 0.1 select_reduce_fusion.1
  92.1 0.0 copy-start.1
  92.1 0.1 reshape.65
  92.2 0.7 select_reduce_fusion.2
  92.9 0.5 dynamic-slice_bitcast_fusion.index_ref
  93.4 0.1 pad_add_fusion.meta
  93.5 0.0 copy-done
  93.5 0.0 copy-done.2
  93.5 1.4 copy-done.4
  94.9 1.6 attend.1
  96.5 0.0 copy-done.1
  96.5 0.0 copy-start.3
  96.5 0.7 copy-done.3
  97.2 0.7 copy-done.5
  97.9 0.6 copy-done.6
  98.5 53.1 %back.1 = (bf16[384,512]{1,0:T(8,128)(2,1)}, bf16[384,256]{1,0:T(8,128)(2,1)}, bf16[384,128]{1,0:T(8,128)(2,1)}, f32[384,64]{1,0:T(8,128)}) custom-call(s32[1,384]{1,0:T(1,128)} %copy-done.1, bf16[384,256]{1,0:T(8,128)(2,1)} %get-tuple-element.37.q_ref, bf16[2,8,384,128]{3,2,1,0:T(8,128)(2,1)} %gather_kv.1.kv_ref, bf16[384,256]{1,0:T(8,128)(2,1)} %copy-done.3, ...), custom_call_target="tpu_custom_call" | custom-call | flops 30000001024 | bytes 100000000 | tf_op jit(solution)/shard_map/back/pallas_call | solution.py:1233
  151.6 4.5 %middle.1 = (bf16[2,384,128]{2,1,0:T(8,128)(2,1)}, bf16[8,64,1152]{2,1,0:T(8,128)(2,1)}) custom-call(s32[3]{0:T(128)} %dynamic-slice_bitcast_fusion.index_ref, bf16[384,512]{1,0:T(8,128)(2,1)} %cot.3, bf16[2,384,128]{2,1,0:T(8,128)(2,1)} %bitcast.15, f32[384,64]{1,0:T(8,128)} %get-tuple-element.45.low_out_ref, bf16[384,256]{1,0:T(8,128)(2,1)} %copy-done.3, ...), custom_call_target="tpu_custom_call" | custom-call | flops 1000000000 | bytes 6000000 | tf_op jit(solution)/shard_map/middle/pallas_call | solution.py:1297
  156.1 13.3 %all-to-all-start = ((bf16[8,64,1152]{2,1,0:T(8,128)(2,1)}), bf16[8,64,1152]{2,1,0:T(8,128)(2,1)S(1)}, u32[]{:S(2)}, u32[]{:S(2)}) async-start(bf16[8,64,1152]{2,1,0:T(8,128)(2,1)} %get-tuple-element.51), calls=%async_computation | async-start | bytes 2359296 | tf_op jit(solution)/shard_map/all_to_all | solution.py:1480
  169.4 52.9 %tail.1 = (bf16[384,512]{1,0:T(8,128)(2,1)}, bf16[768,128]{1,0:T(8,128)(2,1)}, bf16[8,128,512]{2,1,0:T(8,128)(2,1)}, bf16[8,256,128]{2,1,0:T(8,128)(2,1)}) custom-call(s32[24]{0:T(128)} %tenant.3, s32[32]{0:T(128)} %store_row.3, bf16[768,128]{1,0:T(8,128)(2,1)} %bitcast.22, bf16[3,128,512]{2,1,0:T(8,128)(2,1)} %get-tuple-element.49.xs, ...), custom_call_target="tpu_custom_call" | custom-call | flops 30000001024 | bytes 100000000 | tf_op jit(solution)/shard_map/tail/pallas_call | solution.py:844
  222.4 0.0 all-to-all-done.arrived
  222.4 1.0 copy-done.7
  223.4 6.8 %to_store.1 = (f32[4,192,512]{2,1,0:T(8,128)}, f32[4,64,256]{2,1,0:T(8,128)}, f32[4,64,128]{2,1,0:T(8,128)}, f32[4,64,256]{2,1,0:T(8,128)}, f32[4,64,512]{2,1,0:T(8,128)}) custom-call(s32[8]{0:T(128)} %get-tuple-element.59.row_ref, bf16[8,64,1152]{2,1,0:T(8,128)(2,1)} %copy-done.7, bf16[8,128,512]{2,1,0:T(8,128)(2,1)} %get-tuple-element.52.x_got, ...), custom_call_target="tpu_custom_call" | custom-call | bytes 6000000 | tf_op jit(solution)/shard_map/to_store/pallas_call | solution.py:1360
  230.2 0.7 copy.22
  230.9 0.7 copy.23
  (13 shorter events, 0.0 us)
Async XLA Ops:
  74.5 18.9 %copy-start = (bf16[3,64,2688]{2,1,0:T(8,128)(2,1)S(1)}, bf16[3,64,2688]{2,1,0:T(8,128)(2,1)}, u32[]{:S(2)}) copy-start(bf16[3,64,2688]{2,1,0:T(8,128)(2,1)} %get-tuple-element.36.maps) | copy-start | bytes 3096580
  74.5 18.9 %copy-start.2 = (bf16[384,256]{1,0:T(8,128)(2,1)S(1)}, bf16[384,256]{1,0:T(8,128)(2,1)}, u32[]{:S(2)}) copy-start(bf16[384,256]{1,0:T(8,128)(2,1)} %get-tuple-element.37.q_ref) | copy-start | bytes 589828
  92.1 4.4 %copy-start.1 = (s32[1,384]{1,0:T(1,128)}, s32[1,384]{1,0:T(1,128)S(1)}, u32[]{:S(2)}) copy-start(s32[1,384]{1,0:T(1,128)S(1)} %broadcast_in_dim.49.start_ref) | copy-start | bytes 4612
  93.5 1.4 copy-start.4
  96.5 0.7 copy-start.3
  97.2 0.7 copy-start.5
  97.9 0.6 copy-start.6
  156.1 66.3 %all-to-all-start = ((bf16[8,64,1152]{2,1,0:T(8,128)(2,1)}), bf16[8,64,1152]{2,1,0:T(8,128)(2,1)S(1)}, u32[]{:S(2)}, u32[]{:S(2)}) async-start(bf16[8,64,1152]{2,1,0:T(8,128)(2,1)} %get-tuple-element.51), calls=%async_computation | async-start | bytes 2359296 | tf_op jit(solution)/shard_map/all_to_all | solution.py:1480
  222.3 7.9 %copy-start.8 = (bf16[384,512]{1,0:T(8,128)(2,1)S(1)}, bf16[384,512]{1,0:T(8,128)(2,1)}, u32[]{:S(2)}) copy-start(bf16[384,512]{1,0:T(8,128)(2,1)} %get-tuple-element.74) | copy-start | bytes 1179652
  222.3 8.6 %copy-start.9 = (bf16[384,512]{1,0:T(8,128)(2,1)S(1)}, bf16[384,512]{1,0:T(8,128)(2,1)}, u32[]{:S(2)}) copy-start(bf16[384,512]{1,0:T(8,128)(2,1)} %get-tuple-element.75) | copy-start | bytes 1179652
  222.4 1.0 copy-start.7
where the time goes:
time: 233 us; the launch traced here: 232 us
  Pallas kernels  204 us (88%)
  starting transfers between devices  13.3 us (6%)
  local copies, waits for them, and re-layouts  6.49 us (3%)
  other arithmetic  4.76 us (2%)
  between operations  2.73 us (1%)
    pallas_call x1, Pallas kernels, front(): pl.pallas_call(functools.partial(front_body, dim, n_ctx, n_tp), out_shape...  65.1 us
    pallas_call x1, Pallas kernels, back(): pl.pallas_call(functools.partial(back_body, dim, n_ctx, n_tp), out_shape=...  53.1 us
    pallas_call x1, Pallas kernels, tail(): pl.pallas_call(functools.partial(tail_body, dim, n_ctx, n), out_shape=(ja...  52.9 us
    pallas_call x1, Pallas kernels, gather_kv(): pl.pallas_call(functools.partial(gather_kv_body, n), out_shape=jax.ShapeD...  17.5 us
    all_to_all x1, starting transfers between devices, body(): lax.all_to_all(sent, 'ctx', split_axis=0, concat_axis=0, tiled=True)  13.3 us
    pallas_call x1, Pallas kernels, to_store(): pl.pallas_call(functools.partial(store_body, dim), out_shape=tuple((jax.S...  6.78 us
    unnamed x22, local copies, waits for them, and re-layouts  5.87 us
  transfers between devices with their start and end apart: 1, of which 0 were waited for; matrix products, arithmetic and copies ran while one was open for 0% of the time, Pallas kernels for 23%

commit v1 on v0

--- a/solution.py
+++ b/solution.py
@@ -631,10 +631,11 @@
             ).astype(BF16)
             self.near_copy(r, way).start()
 
-    def begin(self):
+    def begin(self, between=lambda: None):
         self.multiply(0, 0, 2)
         self.multiply(1, 0, 2)
         self.go_far(0)
+        between()
         self.multiply(0, 2, self.chips)
         self.go_far(1)
         self.multiply(1, 2, self.chips)
@@ -691,6 +692,21 @@
         )
 
 
+def chooser(dim, n_ctx, tenant, store_row):
+    row = lax.axis_index("ctx")
+    tenants = store_row.shape[0] // n_ctx
+    owners = [store_row[tenant[row * dim.blocks + b]] // tenants for b in range(dim.blocks)]
+
+    def chosen(k, values):
+        owner = lax.rem(row + k, n_ctx)
+        value = values[0]
+        for b in range(1, dim.blocks):
+            value = jnp.where(owners[b] == owner, values[b], value)
+        return value
+
+    return chosen
+
+
 def greet(n_ctx, n_tp):
     c = lax.axis_index("ctx")
     t = lax.axis_index("tp")
@@ -711,27 +727,27 @@
     tenant,
     store_row,
     part,
-    xs,
-    maps,
     gq,
     gkv,
     wq_hbm,
     wkv_hbm,
+    maps_hbm,
+    sent,
     o_ref,
     low_grad,
-    x_got,
     low_got,
+    arrived,
     wq,
     wkv,
+    maps,
     gq_t,
     gkv_t,
-    x_give,
     low_give,
     load_sem,
-    x_send,
-    x_recv,
     low_send,
     low_recv,
+    up_send,
+    up_recv,
     *refs,
 ):
     row = lax.axis_index("ctx")
@@ -741,7 +757,12 @@
         pltpu.make_async_copy(wq_hbm, wq, load_sem.at[0]),
         pltpu.make_async_copy(wkv_hbm, wkv, load_sem.at[1]),
     ]
-    for load in loads:
+    later = [
+        pltpu.make_async_copy(maps_hbm, maps, load_sem.at[2]),
+        pltpu.make_async_copy(sent.at[row], arrived.at[row], load_sem.at[3]),
+        pltpu.make_async_copy(low_give.at[0], low_got.at[row], load_sem.at[4]),
+    ]
+    for load in loads + later[:2]:
         load.start()
     sums = SumTp(n, part, low_grad, *refs[:6])
     wide = dim.width // 2
@@ -751,15 +772,7 @@
         return nn(wq[at, :], gq_t[...]) + nn(wkv[at, :], gkv_t[...])
 
     scatter = ScatterTp(n, product, refs[6:])
-    tenants = store_row.shape[0] // n_ctx
-    owners = [store_row[tenant[row * dim.blocks + b]] // tenants for b in range(dim.blocks)]
-
-    def chosen(k, values):
-        owner = lax.rem(row + k, n_ctx)
-        value = values[0]
-        for b in range(1, dim.blocks):
-            value = jnp.where(owners[b] == owner, values[b], value)
-        return value
+    chosen = chooser(dim, n_ctx, tenant, store_row)
 
     def hand(k, source, target, send, arrive):
         return pltpu.make_async_remote_copy(
@@ -771,11 +784,20 @@
             device_id_type=MESH,
         )
 
-    def hand_x():
+    def hand_all_up():
         for k in range(1, n_ctx):
-            x_give[k] = chosen(k, [xs[b] for b in range(dim.blocks)])
-            hand(k, x_give, x_got, x_send, x_recv).start()
-        x_got[row] = chosen(0, [xs[b] for b in range(dim.blocks)])
+            hand_up(k).start()
+
+    def hand_up(k):
+        peer = lax.rem(row + k, n_ctx)
+        return pltpu.make_async_remote_copy(
+            src_ref=sent.at[peer],
+            dst_ref=arrived.at[row],
+            send_sem=up_send.at[k],
+            recv_sem=up_recv.at[k],
+            device_id=(peer, me),
+            device_id_type=MESH,
+        )
 
     def lows(b):
         return jnp.concatenate(
@@ -792,7 +814,8 @@
         for k in range(1, n_ctx):
             low_give[k] = chosen(k, values)
             hand(k, low_give, low_got, low_send, low_recv).start()
-        low_got[row] = chosen(0, values)
+        low_give[0] = chosen(0, values)
+        later[2].start()
 
     def finish(r):
         total = scatter.total(r).T
@@ -818,24 +841,26 @@
     sums.start()
     for load in loads:
         load.wait()
-    scatter.begin()
-    hand_x()
+    scatter.begin(hand_all_up)
+    scatter.go_near(0)
     sums.middle()
-    for r in range(2):
-        scatter.go_near(r)
+    scatter.go_near(1)
     hand_low()
-    for r in range(2):
-        scatter.go_last(r)
-    for r in range(2):
-        finish(r)
+    later[0].wait()
+    scatter.go_last(0)
+    scatter.go_last(1)
+    finish(0)
+    finish(1)
     for k in range(1, n_ctx):
-        hand(k, x_give, x_got, x_send, x_recv).wait()
         hand(k, low_give, low_got, low_send, low_recv).wait()
+        hand_up(k).wait()
+    for copy in later[1:]:
+        copy.wait()
     sums.drain()
     scatter.drain()
 
 
-def tail(dim, tenant, store_row, part, xs, maps, grad_q, grad_kv, wq, wkv, collective_id):
+def tail(dim, tenant, store_row, part, grad_q, grad_kv, wq, wkv, maps, sent, collective_id):
     n = lax.axis_size("tp")
     n_ctx = lax.axis_size("ctx")
     low_shape = (n_ctx, 2 * BLK, HEAD)
@@ -846,19 +871,19 @@
         out_shape=(
             jax.ShapeDtypeStruct((dim.rows, dim.width), BF16),
             jax.ShapeDtypeStruct(part.shape, BF16),
-            jax.ShapeDtypeStruct((n_ctx, BLK, dim.width), BF16),
             jax.ShapeDtypeStruct(low_shape, BF16),
+            jax.ShapeDtypeStruct(sent.shape, BF16),
         ),
-        in_specs=[smem, smem] + [vmem_spec()] * 5 + [any_spec()] * 2,
-        out_specs=(vmem_spec(),) * 4,
+        in_specs=[smem, smem] + [vmem_spec()] * 3 + [any_spec()] * 4,
+        out_specs=(vmem_spec(),) * 2 + (any_spec(),) * 2,
         scratch_shapes=[
             pltpu.VMEM(wq.shape, BF16),
             pltpu.VMEM(wkv.shape, BF16),
+            pltpu.VMEM(maps.shape, BF16),
             pltpu.VMEM(grad_q.shape[::-1], BF16),
             pltpu.VMEM(grad_kv.shape[::-1], BF16),
-            pltpu.VMEM((n_ctx, BLK, dim.width), BF16),
             pltpu.VMEM(low_shape, BF16),
-            sems((2,)),
+            sems((5,)),
         ]
         + [sems((n_ctx,))] * 4
         + SumTp.scratch(n, part.shape, BF16)
@@ -868,7 +893,7 @@
         ),
         cost_estimate=cost(3e10, 1e8),
         name="tail",
-    )(tenant, store_row, part, xs, maps, grad_q, grad_kv, wq, wkv)
+    )(tenant, store_row, part, grad_q, grad_kv, wq, wkv, maps, sent)
 
 
 def finalize_body(dim, xq, xkv, low, maps, ctab, stab, q_out, kv_out, delta_out):
@@ -1053,22 +1078,29 @@
     dim,
     n_ctx,
     n_tp,
+    tenant,
+    store_row,
     start_ref,
     q_ref,
-    kv_ref,
     o_ref,
     lse_ref,
     low_part,
     o_delta,
     ctab,
     stab,
-    maps,
+    xs,
+    kv_hbm,
+    maps_hbm,
     cot_hbm,
     wo_hbm,
     out_ref,
     dq_ref,
     gkv_ref,
     low_out,
+    x_got,
+    x_give,
+    kv_ref,
+    maps,
     cot_ref,
     wo_ref,
     dkv_ref,
@@ -1083,6 +1115,8 @@
     recv_a,
     send_b,
     recv_b,
+    x_send,
+    x_recv,
     *refs,
 ):
     c = lax.axis_index("ctx")
@@ -1095,8 +1129,10 @@
     entered = greet(n_ctx, n_tp)
     load_wo = pltpu.make_async_copy(wo_hbm, wo_ref, load_sem.at[0])
     load_cot = pltpu.make_async_copy(cot_hbm, cot_ref, load_sem.at[1])
-    load_wo.start()
-    load_cot.start()
+    load_kv = pltpu.make_async_copy(kv_hbm, kv_ref, load_sem.at[2])
+    load_maps = pltpu.make_async_copy(maps_hbm, maps, load_sem.at[3])
+    for load in (load_wo, load_cot, load_kv, load_maps):
+        load.start()
     sums = SumTp(n_tp, low_part, low_out, *refs[:6])
     wide = dim.width // 2
 
@@ -1108,10 +1144,32 @@
     entered()
     sums.start()
     load_wo.wait()
-    scatter.begin()
+    chosen = chooser(dim, n_ctx, tenant, store_row)
+    keep_x = pltpu.make_async_copy(x_give.at[0], x_got.at[c], load_sem.at[4])
+
+    def hand_x(k):
+        return pltpu.make_async_remote_copy(
+            src_ref=x_give.at[k],
+            dst_ref=x_got.at[c],
+            send_sem=x_send.at[k],
+            recv_sem=x_recv.at[k],
+            device_id=(lax.rem(c + k, n_ctx), t),
+            device_id_type=MESH,
+        )
+
+    def hand_all_x():
+        for k in range(n_ctx):
+            x_give[k] = chosen(k, [xs[b] for b in range(dim.blocks)])
+            if k == 0:
+                keep_x.start()
+            else:
+                hand_x(k).start()
+
+    scatter.begin(hand_all_x)
     sums.middle()
 
-    load_cot.wait()
+    for load in (load_cot, load_kv, load_maps):
+        load.wait()
     grad[...] = o_delta[...]
 
     def features(g, carry):
@@ -1221,11 +1279,13 @@
         swap(k).wait_send()
     for k in range(1, n_ctx):
         send(k).wait_send()
+        hand_x(k).wait()
+    keep_x.wait()
     sums.drain()
     scatter.drain()
 
 
-def back(dim, start, q, kv, out, lse, low_part, o_delta, ctab, stab, maps, cot_all, wo, collective_id):
+def back(dim, tenant, store_row, start, q, kv, out, lse, low_part, o_delta, ctab, stab, xs, maps, cot_all, wo, collective_id):
     n_ctx = lax.axis_size("ctx")
     n_tp = lax.axis_size("tp")
     rows = dim.rows
@@ -1237,10 +1297,14 @@
             jax.ShapeDtypeStruct(q.shape, BF16),
             jax.ShapeDtypeStruct((rows, HEAD), BF16),
             jax.ShapeDtypeStruct(low_part.shape, F32),
+            jax.ShapeDtypeStruct((n_ctx,) + xs.shape[1:], BF16),
         ),
-        in_specs=[vmem_spec()] * 10 + [any_spec()] * 2,
-        out_specs=(vmem_spec(),) * 4,
+        in_specs=[pl.BlockSpec(memory_space=pltpu.SMEM)] * 2 + [vmem_spec()] * 9 + [any_spec()] * 4,
+        out_specs=(vmem_spec(),) * 4 + (any_spec(),),
         scratch_shapes=[
+            pltpu.VMEM((n_ctx,) + xs.shape[1:], BF16),
+            pltpu.VMEM(kv.shape, BF16),
+            pltpu.VMEM(maps.shape, BF16),
             pltpu.VMEM(cot_all.shape, BF16),
             pltpu.VMEM(wo.shape, BF16),
             pltpu.VMEM(kv.shape, BF16),
@@ -1250,9 +1314,9 @@
             pltpu.VMEM((n_ctx, rows, HEAD), BF16),
             pltpu.VMEM((n_ctx, rows, HEAD), BF16),
             pltpu.VMEM((n_ctx, rows, HEAD), BF16),
-            sems((2,)),
+            sems((5,)),
         ]
-        + [sems((n_ctx,))] * 4
+        + [sems((n_ctx,))] * 6
         + SumTp.scratch(n_tp, low_part.shape, F32)
         + ScatterTp.scratch(n_tp, rows, dim.width // 2, 2),
         compiler_params=pltpu.CompilerParams(
@@ -1260,7 +1324,7 @@
         ),
         cost_estimate=cost(3e10, 1e8),
         name="back",
-    )(start, q, kv, out, lse, low_part, o_delta, ctab, stab, maps, cot_all, wo)
+    )(tenant, store_row, start, q, out, lse, low_part, o_delta, ctab, stab, xs, kv, maps, cot_all, wo)
 
 
 def middle_body(
@@ -1323,49 +1387,37 @@
 
 
 def store_body(dim, row_ref, arrived, x_got, low_got, down, q_up, kv_up, o_down, o_up):
-    i = pl.program_id(0)
-
-    @pl.when(i == 0)
-    def _():
-        for ref in (down, q_up, kv_up, o_down, o_up):
-            ref[...] = jnp.zeros_like(ref)
-
-    row = row_ref[i]
-
-    @pl.when(row >= 0)
-    def _():
-        base = dim.ou.start
-
-        def piece(at):
-            return arrived[0, :, at.start - base : at.stop - base].astype(F32)
-
-        x = x_got[0]
-        down[row, 0 : 2 * RANK, :] += nn(low_got[0, :BLK, :].T, x)
-        down[row, 2 * RANK :, :] += nn(low_got[0, BLK:, :].T[:RANK], x)
-        q_up[row] += piece(dim.qu)
-        kv_up[row] += piece(dim.kvu)
-        o_down[row] += piece(dim.od)
-        o_up[row] += piece(dim.ou)
+    for ref in (down, q_up, kv_up, o_down, o_up):
+        ref[...] = jnp.zeros_like(ref)
+    base = dim.ou.start
+
+    def one(i, carry):
+        row = row_ref[i]
+
+        @pl.when(row >= 0)
+        def _():
+            def piece(at):
+                return arrived[i, :, at.start - base : at.stop - base].astype(F32)
+
+            x = x_got[i]
+            down[row, 0 : 2 * RANK, :] += nn(low_got[i, :BLK, :].T, x)
+            down[row, 2 * RANK :, :] += nn(low_got[i, BLK:, :].T[:RANK], x)
+            q_up[row] += piece(dim.qu)
+            kv_up[row] += piece(dim.kvu)
+            o_down[row] += piece(dim.od)
+            o_up[row] += piece(dim.ou)
+
+        return carry
+
+    lax.fori_loop(0, arrived.shape[0], one, 0)
 
 
 def to_store(dim, rows, arrived, x_got, low_got, shapes):
-    count = arrived.shape[0]
-
-    def whole(shape):
-        return pl.BlockSpec(shape, lambda i, idx: (0, 0, 0))
-
-    def one(array):
-        return pl.BlockSpec((1,) + array.shape[1:], lambda i, idx: (i, 0, 0))
-
     return pl.pallas_call(
         functools.partial(store_body, dim),
         out_shape=tuple(jax.ShapeDtypeStruct(s, F32) for s in shapes),
-        grid_spec=pltpu.PrefetchScalarGridSpec(
-            num_scalar_prefetch=1,
-            grid=(count,),
-            in_specs=[one(arrived), one(x_got), one(low_got)],
-            out_specs=tuple(whole(s) for s in shapes),
-        ),
+        in_specs=[pl.BlockSpec(memory_space=pltpu.SMEM)] + [vmem_spec()] * 3,
+        out_specs=tuple(vmem_spec() for s in shapes),
         cost_estimate=cost(0, 6e6),
         name="to_store",
     )(rows, arrived, x_got, low_got)
@@ -1445,8 +1497,10 @@
     kv_all = gather_kv(keyval, 1)
     attn, lse, low_part = attend(dim, meta, start, query, kv_all, maps)
 
-    output, grad_q, grad_kv, low_out = back(
+    output, grad_q, grad_kv, low_out, x_got = back(
         dim,
+        tenant_per_block,
+        tenant_store_row,
         start,
         query,
         kv_all,
@@ -1456,6 +1510,7 @@
         o_delta,
         ctab,
         stab,
+        x_mine,
         maps,
         cot_all,
         output_projection,
@@ -1464,20 +1519,19 @@
     low_grad_part, sent = middle(
         dim, my_owner, ctx_count, output_cotangent, low_in, low_out, attn, grad_q, grad_kv, maps
     )
-    hidden_input_gradient, unused, x_got, low_got = tail(
+    hidden_input_gradient, unused, low_got, returned = tail(
         dim,
         tenant_per_block,
         tenant_store_row,
         low_grad_part.reshape(2 * rows_dev, HEAD),
-        x_mine,
-        maps,
         grad_q,
         grad_kv,
         query_projection,
         key_value_projection,
+        maps,
+        sent,
         3,
     )
-    returned = lax.all_to_all(sent, "ctx", split_axis=0, concat_axis=0, tiled=True)
     grads = to_store(dim, served_row, returned, x_got, low_got, [s.shape for s in stores])
     return (
         output,

time: 233 us -> 218 us (0.936)
  starting transfers between devices: 13.3 us -> 0 us
    all_to_all x1 -> x0, starting transfers between devices: 13.3 us -> none  [body(): lax.all_to_all(sent, 'ctx', split_axis=0, concat_axis=0, tiled=True)]
    pallas_call x1, Pallas kernels: 52.9 us -> 57 us  [tail(): pl.pallas_call(functools.partial(tail_body, dim, n_ctx, n), out_shape=(ja...]
    pallas_call x1, Pallas kernels: 53.1 us -> 50.3 us  [back(): pl.pallas_call(functools.partial(back_body, dim, n_ctx, n_tp), out_shape=...]
    unnamed x22 -> x24, local copies, waits for them, and re-layouts: 5.87 us -> 4.84 us
  transfers between devices with their start and end apart: 1 -> 0, of which waited for: 0 -> 0; matrix products, arithmetic and copies ran while one was open for 0% -> 0% of each run, Pallas kernels for 23% -> 0%
where the time goes in v1:
time: 218 us; the launch traced here: 216 us
  Pallas kernels  203 us (93%)
  local copies, waits for them, and re-layouts  5.44 us (2%)
  other arithmetic  4.06 us (2%)
  between operations  2.73 us (1%)
    pallas_call x1, Pallas kernels, front(): pl.pallas_call(functools.partial(front_body, dim, n_ctx, n_tp), out_shape...  65.2 us
    pallas_call x1, Pallas kernels, tail(): pl.pallas_call(functools.partial(tail_body, dim, n_ctx, n), out_shape=(ja...  57 us
    pallas_call x1, Pallas kernels, back(): pl.pallas_call(functools.partial(back_body, dim, n_ctx, n_tp), out_shape=...  50.3 us
    pallas_call x1, Pallas kernels, gather_kv(): pl.pallas_call(functools.partial(gather_kv_body, n), out_shape=jax.ShapeD...  17.5 us
    unnamed x24, local copies, waits for them, and re-layouts  4.84 us
    pallas_call x1, Pallas kernels, to_store(): pl.pallas_call(functools.partial(store_body, dim), out_shape=tuple((jax.S...  4.52 us
    pallas_call x1, Pallas kernels, middle(): pl.pallas_call(functools.partial(middle_body, dim), out_shape=(jax.ShapeD...  4.44 us

profile of v1, /device:TPU:0, one launch (start us, length us, event | category | flops | bytes accessed | tf_op | source)
XLA Modules:
  0.0 215.6 jit_solution(9406043070512526349)
XLA Ops:
  0.6 0.8 reduce-window.8
  1.5 0.6 fusion.4
  4.1 0.1 pad_add_fusion.meta
  4.2 0.1 compare_select_fusion.1
  4.2 1.5 fusion
  5.8 65.2 %front.1 = (bf16[3,64,2688]{2,1,0:T(8,128)(2,1)}, bf16[768,128]{1,0:T(8,128)(2,1)}, f32[384,256]{1,0:T(8,128)}, f32[384,128]{1,0:T(8,128)}, bf16[16,384,512]{2,1,0:T(8,128)(2,1)}, /*index=5*/bf16[3,128,512]{2,1,0:T(8,128)(2,1)}) custom-call(s32[24]{0:T(128)} %tenant.5, s32[32]{0:T(128)} %store_row.5, bf16[4,192,512]{2,1,0:T(8,128)(2,1)} %bitcast.18, ...), custom_call_target="tpu_custom_call" | custom-call | flops 30000001024 | bytes 100000000 | tf_op jit(solution)/shard_map/front/pallas_call | solution.py:387
  70.9 2.8 %finalize.1 = (bf16[384,256]{1,0:T(8,128)(2,1)}, bf16[384,128]{1,0:T(8,128)(2,1)}, f32[384,256]{1,0:T(8,128)}) custom-call(f32[384,256]{1,0:T(8,128)} %get-tuple-element.34.xq, f32[384,128]{1,0:T(8,128)} %get-tuple-element.35.xkv, bf16[2,384,128]{2,1,0:T(8,128)(2,1)} %bitcast.14, bf16[3,64,2688]{2,1,0:T(8,128)(2,1)} %get-tuple-element.37.maps.maps_hbm, ...), custom_call_target="tpu_custom_call" | custom-call | flops 100000000 | bytes 4000000 | tf_op jit(solution)/shard_map/finalize/pallas_call | solution.py:926
  73.8 17.5 %gather_kv.1.kv_ref.kv_hbm = bf16[2,8,384,128]{3,2,1,0:T(8,128)(2,1)} custom-call(bf16[384,128]{1,0:T(8,128)(2,1)} %get-tuple-element.39.x_ref), custom_call_target="tpu_custom_call" | custom-call | flops 3000000000 | bytes 30000000 | tf_op jit(solution)/shard_map/gather_kv/pallas_call | solution.py:996
  91.3 0.1 select_reduce_fusion.1
  91.4 0.0 copy-done
  91.4 0.0 copy-done.2
  91.4 0.0 copy-start.4
  91.4 1.4 copy-done.4
  92.8 1.6 attend.1
  94.4 0.0 copy-done.1
  94.4 0.0 copy-start.3
  94.4 0.7 copy-done.3
  95.1 0.7 copy-done.5
  95.8 0.6 copy-done.6
  96.4 50.3 %back.1 = (bf16[384,512]{1,0:T(8,128)(2,1)}, bf16[384,256]{1,0:T(8,128)(2,1)}, bf16[384,128]{1,0:T(8,128)(2,1)}, f32[384,64]{1,0:T(8,128)}, bf16[8,128,512]{2,1,0:T(8,128)(2,1)}) custom-call(s32[24]{0:T(128)} %tenant.5, s32[32]{0:T(128)} %store_row.5, s32[1,384]{1,0:T(1,128)} %copy-done.1, bf16[384,256]{1,0:T(8,128)(2,1)} %get-tuple-element.38.q_ref, ...), custom_call_target="tpu_custom_call" | custom-call | flops 30000001024 | bytes 100000000 | tf_op jit(solution)/shard_map/back/pallas_call | solution.py:1293
  146.7 0.0 copy-done.9
  146.7 0.2 select_reduce_fusion
  146.9 0.1 reshape.65
  147.0 0.6 select_reduce_fusion.2
  147.6 0.5 dynamic-slice_bitcast_fusion.index_ref
  148.1 4.4 %middle.1 = (bf16[2,384,128]{2,1,0:T(8,128)(2,1)}, bf16[8,64,1152]{2,1,0:T(8,128)(2,1)}) custom-call(s32[3]{0:T(128)} %dynamic-slice_bitcast_fusion.index_ref, bf16[384,512]{1,0:T(8,128)(2,1)} %cot.3, bf16[2,384,128]{2,1,0:T(8,128)(2,1)} %bitcast.15, f32[384,64]{1,0:T(8,128)} %get-tuple-element.47.low_out_ref, bf16[384,256]{1,0:T(8,128)(2,1)} %copy-done.3, ...), custom_call_target="tpu_custom_call" | custom-call | flops 1000000000 | bytes 6000000 | tf_op jit(solution)/shard_map/middle/pallas_call | solution.py:1361
  152.6 57.0 %tail.1 = (bf16[384,512]{1,0:T(8,128)(2,1)}, bf16[768,128]{1,0:T(8,128)(2,1)}, bf16[8,256,128]{2,1,0:T(8,128)(2,1)}, bf16[8,64,1152]{2,1,0:T(8,128)(2,1)}) custom-call(s32[24]{0:T(128)} %tenant.5, s32[32]{0:T(128)} %store_row.5, bf16[768,128]{1,0:T(8,128)(2,1)} %bitcast.22, bf16[384,256]{1,0:T(8,128)(2,1)} %get-tuple-element.48.grad_q.gq, ...), custom_call_target="tpu_custom_call" | custom-call | flops 30000001024 | bytes 100000000 | tf_op jit(solution)/shard_map/tail/pallas_call | solution.py:869
  209.6 0.0 copy-start.7
  209.6 0.0 copy-start.8
  209.6 4.5 %to_store.1 = (f32[4,192,512]{2,1,0:T(8,128)}, f32[4,64,256]{2,1,0:T(8,128)}, f32[4,64,128]{2,1,0:T(8,128)}, f32[4,64,256]{2,1,0:T(8,128)}, f32[4,64,512]{2,1,0:T(8,128)}) custom-call(s32[8]{0:T(128)} %get-tuple-element.61.row_ref, bf16[8,64,1152]{2,1,0:T(8,128)(2,1)} %get-tuple-element.53.arrived, bf16[8,128,512]{2,1,0:T(8,128)(2,1)} %get-tuple-element.54.x_got, ...), custom_call_target="tpu_custom_call" | custom-call | bytes 6000000 | tf_op jit(solution)/shard_map/to_store/pallas_call | solution.py:1416
  214.1 0.7 copy.22
  214.8 0.7 copy.23
  (13 shorter events, 0.0 us)
Async XLA Ops:
  73.8 17.6 %copy-start = (bf16[3,64,2688]{2,1,0:T(8,128)(2,1)S(1)}, bf16[3,64,2688]{2,1,0:T(8,128)(2,1)}, u32[]{:S(2)}) copy-start(bf16[3,64,2688]{2,1,0:T(8,128)(2,1)} %get-tuple-element.37.maps.maps_hbm) | copy-start | bytes 3096580
  73.8 17.6 %copy-start.2 = (bf16[384,256]{1,0:T(8,128)(2,1)S(1)}, bf16[384,256]{1,0:T(8,128)(2,1)}, u32[]{:S(2)}) copy-start(bf16[384,256]{1,0:T(8,128)(2,1)} %get-tuple-element.38.q_ref) | copy-start | bytes 589828
  91.4 1.4 copy-start.4
  92.8 1.6 copy-start.1
  94.4 0.7 copy-start.3
  95.1 0.7 copy-start.5
  95.8 0.6 copy-start.6
  96.4 50.3 %copy-start.9 = (s32[24]{0:T(128)S(1)}, s32[24]{0:T(128)}, u32[]{:S(2)}) copy-start(s32[24]{0:T(128)} %tenant.5) | copy-start | bytes 292
  96.4 50.3 %copy-start.10 = (s32[32]{0:T(128)S(1)}, s32[32]{0:T(128)}, u32[]{:S(2)}) copy-start(s32[32]{0:T(128)} %store_row.5) | copy-start | bytes 388
  209.6 4.5 %copy-start.7 = (bf16[384,512]{1,0:T(8,128)(2,1)S(1)}, bf16[384,512]{1,0:T(8,128)(2,1)}, u32[]{:S(2)}) copy-start(bf16[384,512]{1,0:T(8,128)(2,1)} %get-tuple-element.76) | copy-start | bytes 1179652
  209.6 5.3 %copy-start.8 = (bf16[384,512]{1,0:T(8,128)(2,1)S(1)}, bf16[384,512]{1,0:T(8,128)(2,1)}, u32[]{:S(2)}) copy-start(bf16[384,512]{1,0:T(8,128)(2,1)} %get-tuple-element.77) | copy-start | bytes 1179652
